TPU v7x, 32 devices: a whole 2x2x4 slice. The times are simulated.
32 devices in a mesh: grp: 4 (over x, core), mem: 8 (over z, y).
Axes of the slice: x: 2, y: 2, z: 4, core: 2. Of those that a mesh axis runs over, the one named last changes fastest.
Arguments:
- perturb: float32 [32, 1024, 1024], P(('grp', 'mem')), may hold values from -0.1875 to 0.1875
- touched_vertex_index: int32 [32, 4, 64], P(('grp', 'mem')), may hold values from 0 to 1023
- proposed_spin_values: int32 [32, 4, 64], P(('grp', 'mem')), may hold values from 0 to 1
- accept: int32 [32, 4, 64], P(('grp', 'mem')), may hold values 0 or 1
- vertex_site_index: int32 [32, 1024], P(('grp', 'mem')), may hold values from 0 to 63
- vertex_time_index: int32 [32, 1024], P(('grp', 'mem')), may hold values from 0 to 4095
- left_proj: float32 [64, 1024], replicated, may hold values from -0.06 to 0.06
- right_proj: float32 [64, 1024], replicated, may hold values from -0.06 to 0.06
- weights: float32 [32], P(('grp', 'mem')), may hold values from 0.3 to 3
- routing: int32 [32, 1], P(('grp', 'mem')), may hold values from 0 to 7; in each aligned block of 8 rows (0 to 7, 8 to 15, ...) at most 2 rows name the same one
- vertex_function_total: float32 [16, 4096, 4096], P('grp', 'mem'), may hold values from -6 to 6
Outputs:
- four_point_out: float32 [16, 4096, 4096], P('grp', 'mem')
Inputs may be any that keep to these rules, and one draw needn't show every extreme that they name: `routing`: among the 8 walkers of one group no member index is named by more than 2 walkers, and in some group one index is named by exactly 2.
All inputs are finite; a program needn't handle non-finite values. No bound on the sum of `accept` on one device may be relied on, other than what follows from the above.
Results may differ from a plain program's by a relative error of at most 0.0003.
Values sent between devices are 32-bit elements; how exact they have to be, the bound alone decides.
A program may use at most 128 MiB of HBM per device.

v0:
```python
import jax
import jax.numpy as jnp
from jax import lax
from jax.sharding import PartitionSpec as P

K = 1024
SITES = 64
LEG = 64
Q = 16
TIMES = 4096
UPDATES = 4


EXACT_ARITHMETIC = lax.Precision.HIGHEST


def legendre(time_ids):
    abscissa = (2.0 * time_ids.astype(jnp.float32) + 1.0) / TIMES - 1.0
    polys = [jnp.ones_like(abscissa), abscissa]
    for degree in range(1, LEG - 1):
        polys.append(
            ((2 * degree + 1) * abscissa * polys[degree] - degree * polys[degree - 1])
            / (degree + 1)
        )
    norms = jnp.sqrt(2.0 * jnp.arange(LEG, dtype=jnp.float32) + 1.0)
    return jnp.stack(polys[:LEG], axis=1) * norms[None, :]


def make_onehot(site_ids):
    return (site_ids[:, None] == jnp.arange(SITES, dtype=jnp.int32)[None, :]).astype(jnp.float32)


def project(onehot, polys, table):
    spread = jnp.dot(onehot, table, precision=EXACT_ARITHMETIC, preferred_element_type=jnp.float32)
    return jnp.sum(spread.reshape(-1, LEG, Q) * polys[:, :, None], axis=1)


def transform(onehot, polys, values):
    weighted = (polys[:, :, None] * values[:, None, :]).reshape(-1, LEG * Q)
    summed = jnp.dot(
        onehot.T, weighted, precision=EXACT_ARITHMETIC, preferred_element_type=jnp.float32
    )
    return summed.reshape(SITES, LEG, Q).transpose(2, 0, 1).reshape(Q, SITES * LEG)


def update_walker(perturb, touched_vertex_index, proposed_spin_values, accept):
    matrix = jnp.eye(K, dtype=jnp.float32) + perturb
    gammas = accept.astype(jnp.float32) * jnp.where(proposed_spin_values == 1, 0.6, -0.4).astype(
        jnp.float32
    )
    positions = jnp.arange(K, dtype=jnp.int32)

    def apply_update(update, matrix):
        chosen = touched_vertex_index[update]
        unit_cols = (positions[:, None] == chosen[None, :]).astype(jnp.float32)
        columns = (jnp.take(matrix, chosen, axis=1) - unit_cols) * gammas[update][None, :]
        row_block = jnp.take(matrix, chosen, axis=0)
        return matrix - jnp.dot(
            columns, row_block, precision=EXACT_ARITHMETIC, preferred_element_type=jnp.float32
        )

    return lax.fori_loop(0, UPDATES, apply_update, matrix)


def reduce_measured_rows(rescaled_rows, right_observed, vertex_function_total):
    left_q, right_q = (
        lax.all_to_all(rescaled_rows, "grp", split_axis=1, concat_axis=0, tiled=True),
        lax.all_to_all(right_observed, "grp", split_axis=1, concat_axis=0, tiled=True),
    )
    left_rows = lax.all_to_all(left_q, "mem", split_axis=2, concat_axis=0, tiled=True)
    return vertex_function_total + jnp.einsum(
        "mqr,mqc->qrc",
        left_rows,
        lax.all_gather(right_q, "mem", axis=0, tiled=True),
        precision=EXACT_ARITHMETIC,
    )


def per_device(
    perturb,
    touched_vertex_index,
    proposed_spin_values,
    accept,
    vertex_site_index,
    vertex_time_index,
    left_proj,
    right_proj,
    weights,
    routing,
    vertex_function_total,
):
    matrix = update_walker(perturb[0], touched_vertex_index[0], proposed_spin_values[0], accept[0])
    polys = legendre(vertex_time_index[0])
    onehot = make_onehot(vertex_site_index[0])
    left_vec = project(onehot, polys, left_proj)
    right_vec = project(onehot, polys, right_proj)
    left_image = jnp.dot(
        matrix, left_vec, precision=EXACT_ARITHMETIC, preferred_element_type=jnp.float32
    )
    right_image = jnp.dot(
        matrix.T, right_vec, precision=EXACT_ARITHMETIC, preferred_element_type=jnp.float32
    )
    member_mask = (jnp.arange(lax.axis_size("mem"), dtype=jnp.int32) == routing[0, 0]).astype(
        jnp.float32
    )
    totals = lax.psum(member_mask * weights[0], "mem")
    own_total = jnp.sum(totals * member_mask)
    gamma_factor_list = weights / own_total
    left_observed = transform(onehot, polys, left_image)[None]
    right_observed = transform(onehot, polys, right_image)[None]
    rescaled_rows = left_observed * gamma_factor_list[:, None, None]
    return reduce_measured_rows(rescaled_rows, right_observed, vertex_function_total)


def solution(mesh):
    in_specs = (
        P(("grp", "mem"), None, None),
        P(("grp", "mem"), None, None),
        P(("grp", "mem"), None, None),
        P(("grp", "mem"), None, None),
        P(("grp", "mem"), None),
        P(("grp", "mem"), None),
        P(),
        P(),
        P(("grp", "mem")),
        P(("grp", "mem"), None),
        P("grp", "mem", None),
    )
    out_specs = P("grp", "mem", None)
    return jax.shard_map(
        per_device, mesh=mesh, in_specs=in_specs, out_specs=out_specs, check_vma=False
    )
```

profile of v0, /device:TPU:0, one launch (start us, length us, event | category | flops | bytes accessed | tf_op | source)
XLA Modules:
  0.0 258.7 jit_solution(9554184018250131046)
XLA Ops:
  7.9 4.9 %bitcast_add_fusion = f32[1024,1024]{1,0:T(8,128)} fusion(f32[1,1024,1024]{2,1,0:T(8,128)} %param.13), kind=kLoop, calls=%fused_computation.24 | loop fusion | flops 3145728 | bytes 8388608 | tf_op jit(solution)/shard_map/add | solution.py:47
  12.8 73.0 %while.14 = (s32[]{:T(128)}, f32[1024,1024]{1,0:T(8,128)}, s32[4,64]{1,0:T(4,128)S(1)}, f32[4,64]{1,0:T(4,128)S(1)}, s32[]{:T(128)}) while((s32[]{:T(128)}, f32[1024,1024]{1,0:T(8,128)}, s32[4,64]{1,0:T(4,128)S(1)}, f32[4,64]{1,0:T(4,128)S(1)}, s32[]{:T(128)}) %tuple.131), condition=%wide.region_1.2_spmd.clone, body=%wide.region_0.1_spmd.clone.sunk | while | flops 806749760 | bytes 18357200 | solution.py:62
  12.9 3.0 %gather_fusion.1 = f32[64,1024]{1,0:T(8,128)S(1)} fusion(f32[1024,1024]{1,0:T(8,128)} %get-tuple-element.275, s32[1024]{0:T(1024)S(1)} %pad_clamp_fusion.2), kind=kCustom, calls=%fused_computation.1.clone.clone.1 | custom fusion | bytes 524544 | tf_op jit(solution)/shard_map/while/body/eval_jaxpr/jit(_take)/gather | solution.py:57
  15.9 5.4 %copy.43 = f32[1024,1024]{0,1:T(8,128)} copy(f32[1024,1024]{1,0:T(8,128)} %get-tuple-element.275) | data formatting | bytes 8388608 | tf_op jit(solution)/shard_map/while
  24.2 6.8 %convolution_subtract_fusion.2 = f32[1024,1024]{1,0:T(8,128)} fusion(f32[1024,1024]{1,0:T(8,128)} %get-tuple-element.275, f32[64,1024]{1,0:T(8,128)S(1)} %gather_fusion, f32[64,1024]{1,0:T(8,128)S(1)} %gather_fusion.1, f32[64]{0:T(128)S(1)} %dynamic-slice_bitcast_fusion.2, s32[64]{0:T(128)S(1)} %get-tuple-element.267, ...), kind=kOutput, calls=%fused_computation.3.clone.1 | convolution fusion | flops 806748160 | bytes 8913472 | tf_op jit(solution)/shard_map/while/body/eval_jaxpr/dot_general | solution.py:58
  31.1 3.0 %gather_fusion.1 = f32[64,1024]{1,0:T(8,128)S(1)} fusion(f32[1024,1024]{1,0:T(8,128)} %get-tuple-element.275, s32[1024]{0:T(1024)S(1)} %pad_clamp_fusion.2), kind=kCustom, calls=%fused_computation.1.clone.clone.1 | custom fusion | bytes 524544 | tf_op jit(solution)/shard_map/while/body/eval_jaxpr/jit(_take)/gather | solution.py:57
  34.1 5.4 %copy.43 = f32[1024,1024]{0,1:T(8,128)} copy(f32[1024,1024]{1,0:T(8,128)} %get-tuple-element.275) | data formatting | bytes 8388608 | tf_op jit(solution)/shard_map/while
  39.5 3.0 %gather_fusion = f32[64,1024]{1,0:T(8,128)S(1)} fusion(f32[1024,1024]{0,1:T(8,128)} %copy.43, s32[1024]{0:T(1024)S(1)} %pad_clamp_fusion.2), kind=kCustom, calls=%fused_computation.clone.clone.1 | custom fusion | bytes 524544 | tf_op jit(solution)/shard_map/while/body/eval_jaxpr/jit(_take)/gather | solution.py:56
  42.4 6.8 %convolution_subtract_fusion.2 = f32[1024,1024]{1,0:T(8,128)} fusion(f32[1024,1024]{1,0:T(8,128)} %get-tuple-element.275, f32[64,1024]{1,0:T(8,128)S(1)} %gather_fusion, f32[64,1024]{1,0:T(8,128)S(1)} %gather_fusion.1, f32[64]{0:T(128)S(1)} %dynamic-slice_bitcast_fusion.2, s32[64]{0:T(128)S(1)} %get-tuple-element.267, ...), kind=kOutput, calls=%fused_computation.3.clone.1 | convolution fusion | flops 806748160 | bytes 8913472 | tf_op jit(solution)/shard_map/while/body/eval_jaxpr/dot_general | solution.py:58
  49.3 3.0 %gather_fusion.1 = f32[64,1024]{1,0:T(8,128)S(1)} fusion(f32[1024,1024]{1,0:T(8,128)} %get-tuple-element.275, s32[1024]{0:T(1024)S(1)} %pad_clamp_fusion.2), kind=kCustom, calls=%fused_computation.1.clone.clone.1 | custom fusion | bytes 524544 | tf_op jit(solution)/shard_map/while/body/eval_jaxpr/jit(_take)/gather | solution.py:57
  52.3 5.4 %copy.43 = f32[1024,1024]{0,1:T(8,128)} copy(f32[1024,1024]{1,0:T(8,128)} %get-tuple-element.275) | data formatting | bytes 8388608 | tf_op jit(solution)/shard_map/while
  57.7 3.0 %gather_fusion = f32[64,1024]{1,0:T(8,128)S(1)} fusion(f32[1024,1024]{0,1:T(8,128)} %copy.43, s32[1024]{0:T(1024)S(1)} %pad_clamp_fusion.2), kind=kCustom, calls=%fused_computation.clone.clone.1 | custom fusion | bytes 524544 | tf_op jit(solution)/shard_map/while/body/eval_jaxpr/jit(_take)/gather | solution.py:56
  60.6 6.8 %convolution_subtract_fusion.2 = f32[1024,1024]{1,0:T(8,128)} fusion(f32[1024,1024]{1,0:T(8,128)} %get-tuple-element.275, f32[64,1024]{1,0:T(8,128)S(1)} %gather_fusion, f32[64,1024]{1,0:T(8,128)S(1)} %gather_fusion.1, f32[64]{0:T(128)S(1)} %dynamic-slice_bitcast_fusion.2, s32[64]{0:T(128)S(1)} %get-tuple-element.267, ...), kind=kOutput, calls=%fused_computation.3.clone.1 | convolution fusion | flops 806748160 | bytes 8913472 | tf_op jit(solution)/shard_map/while/body/eval_jaxpr/dot_general | solution.py:58
  67.5 3.0 %gather_fusion.1 = f32[64,1024]{1,0:T(8,128)S(1)} fusion(f32[1024,1024]{1,0:T(8,128)} %get-tuple-element.275, s32[1024]{0:T(1024)S(1)} %pad_clamp_fusion.2), kind=kCustom, calls=%fused_computation.1.clone.clone.1 | custom fusion | bytes 524544 | tf_op jit(solution)/shard_map/while/body/eval_jaxpr/jit(_take)/gather | solution.py:57
  70.5 5.4 %copy.43 = f32[1024,1024]{0,1:T(8,128)} copy(f32[1024,1024]{1,0:T(8,128)} %get-tuple-element.275) | data formatting | bytes 8388608 | tf_op jit(solution)/shard_map/while
  75.9 3.0 %gather_fusion = f32[64,1024]{1,0:T(8,128)S(1)} fusion(f32[1024,1024]{0,1:T(8,128)} %copy.43, s32[1024]{0:T(1024)S(1)} %pad_clamp_fusion.2), kind=kCustom, calls=%fused_computation.clone.clone.1 | custom fusion | bytes 524544 | tf_op jit(solution)/shard_map/while/body/eval_jaxpr/jit(_take)/gather | solution.py:56
  78.8 6.8 %convolution_subtract_fusion.2 = f32[1024,1024]{1,0:T(8,128)} fusion(f32[1024,1024]{1,0:T(8,128)} %get-tuple-element.275, f32[64,1024]{1,0:T(8,128)S(1)} %gather_fusion, f32[64,1024]{1,0:T(8,128)S(1)} %gather_fusion.1, f32[64]{0:T(128)S(1)} %dynamic-slice_bitcast_fusion.2, s32[64]{0:T(128)S(1)} %get-tuple-element.267, ...), kind=kOutput, calls=%fused_computation.3.clone.1 | convolution fusion | flops 806748160 | bytes 8913472 | tf_op jit(solution)/shard_map/while/body/eval_jaxpr/dot_general | solution.py:58
  85.8 3.8 %fusion.28 = f32[1024,1024]{0,1:T(8,128)} fusion(f32[64,1024]{1,0:T(8,128)S(1)} %copy-done, s32[1024]{0:T(1024)S(1)} %bitcast.184), kind=kOutput, calls=%fused_computation.39 | convolution fusion | flops 805371904 | bytes 4460544 | tf_op jit(solution)/shard_map/dot_general | solution.py:34
  89.6 3.8 %fusion.30 = f32[1024,1024]{0,1:T(8,128)} fusion(f32[64,1024]{1,0:T(8,128)S(1)} %copy-done.3, s32[1024]{0:T(1024)S(1)} %bitcast.185), kind=kOutput, calls=%fused_computation.41 | convolution fusion | flops 805371904 | bytes 4460544 | tf_op jit(solution)/shard_map/dot_general | solution.py:34
  94.5 4.7 %multiply_reduce_fusion = (f32[1024,16]{0,1:T(8,128)S(1)}, f32[1024,16]{0,1:T(8,128)S(1)}) fusion(f32[1024,64,16]{0,2,1:T(8,128)} %bitcast.178, f32[1024,64]{0,1:T(8,128)S(1)} %broadcast_multiply_fusion, f32[1024,64,16]{0,2,1:T(8,128)} %bitcast.179), kind=kLoop, calls=%fused_computation.30 | loop fusion | flops 4161536 | bytes 8781824 | tf_op jit(solution)/shard_map/reduce_sum | solution.py:35
  101.5 3.6 %fusion.41 = f32[1024,16]{0,1:T(8,128)S(1)} fusion(f32[1024,1024]{1,0:T(8,128)S(1)} %copy-done.2, f32[1024,16]{0,1:T(8,128)S(1)} %get-tuple-element.111), kind=kOutput, calls=%fused_computation.217 | convolution fusion | flops 201326592 | bytes 4325376 | tf_op jit(solution)/shard_map/dot_general | solution.py:97
  107.7 5.6 %fusion.19 = f32[16,64,64]{2,1,0:T(8,128)S(1)} fusion(f32[64,16,1024]{2,1,0:T(8,128)S(1)} %get-tuple-element.173, s32[1024]{0:T(1024)S(1)} %bitcast.186), kind=kOutput, calls=%fused_computation.35 | convolution fusion | flops 805371904 | bytes 4460544 | tf_op jit(solution)/shard_map/dot_general | solution.py:40
  113.7 10.0 %all_to_all.42 = f32[1,16,4096]{2,0,1:T(1,128)S(1)} all-to-all(f32[1,16,4096]{2,0,1:T(1,128)S(1)} %broadcast_in_dim_reshape.5), channel_id=1, replica_groups=mesh['grp'=4,'mem'=8] {'grp'}, dimensions={1} | all-to-all | bytes 524288 | tf_op jit(solution)/shard_map/all_to_all | solution.py:68
  126.5 21.8 %psum.7 = f32[8]{0:T(128)S(1)} all-reduce(f32[8]{0:T(128)S(1)} %compare_select_fusion.3), channel_id=1, replica_groups=mesh['grp'=4,'mem'=8] {'mem'}, use_global_device_ids=true, to_apply=%region_3.4 | all-reduce | flops 8 | bytes 64 | tf_op jit(solution)/shard_map/psum | solution.py:106
  149.6 7.4 %fusion.25 = f32[16,64,64]{2,1,0:T(8,128)S(1)} fusion(f32[64,16,1024]{2,1,0:T(8,128)} %get-tuple-element.174, f32[]{:T(128)} %bitcast.34, s32[1024]{0:T(1024)S(1)} %bitcast.187), kind=kOutput, calls=%fused_computation.37 | convolution fusion | flops 805437440 | bytes 4460548 | tf_op jit(solution)/shard_map/dot_general | solution.py:40
  157.4 8.8 %all_to_all.43 = f32[1,16,4096]{2,0,1:T(1,128)S(1)} all-to-all(f32[1,16,4096]{2,0,1:T(1,128)S(1)} %mul.18371), channel_id=1, replica_groups=mesh['grp'=4,'mem'=8] {'grp'}, dimensions={1} | all-to-all | bytes 524288 | tf_op jit(solution)/shard_map/all_to_all | solution.py:67
  166.9 5.8 %copy.21 = f32[4,4,4096]{1,0,2:T(4,128)} copy(f32[4,4,4096]{2,1,0:T(4,128)S(1)} %all_to_all.32) | data formatting | bytes 524288 | tf_op jit(solution)/shard_map/all_to_all | solution.py:67
  172.7 11.3 %reshape.1435 = f32[8,1,8192]{2,1,0:T(1,128)S(1)} reshape(f32[4096,4,4]{2,1,0:T(4,128)} %bitcast.176) | data formatting | bytes 524288
  184.0 11.6 %all_to_all.44 = f32[8,1,8192]{2,1,0:T(1,128)S(1)} all-to-all(f32[8,1,8192]{2,1,0:T(1,128)S(1)} %reshape.1435), channel_id=1, replica_groups=mesh['grp'=4,'mem'=8] {'mem'}, dimensions={0} | all-to-all | bytes 524288 | tf_op jit(solution)/shard_map/all_to_all | solution.py:70
  197.4 14.2 %reshape.1436 = f32[4096,4,4]{2,1,0:T(4,128)} reshape(f32[8,8192]{1,0:T(8,128)S(1)} %reduce.2) | data formatting | bytes 524288
  211.6 5.2 %copy.27 = f32[4,4,8,512]{3,2,1,0:T(8,128)S(1)} copy(f32[4,4,8,512]{1,0,3,2:T(4,128)} %bitcast.177) | data formatting | bytes 524288 | tf_op jit(solution)/shard_map/all_to_all | solution.py:70
  217.2 34.5 %convolution_add_fusion = f32[4,512,4096]{2,1,0:T(8,128)} fusion(f32[4,512,4096]{2,1,0:T(8,128)} %param.23, f32[32,4,512]{2,0,1:T(8,128)S(1)} %all_to_all.36, f32[32,4,4096]{2,1,0:T(4,128)} %all-gather.2.cloned.1.call-done), kind=kOutput, calls=%fused_computation.23 | convolution fusion | flops 3229614080 | bytes 69468160 | tf_op jit(solution)/shard_map/mqr,mqc->qrc/dot_general | solution.py:71
  (78 shorter events, 15.7 us)
Async XLA Ops:
  6.5 79.3 %copy-start = (f32[64,1024]{1,0:T(8,128)S(1)}, f32[64,1024]{1,0:T(8,128)}, u32[]{:S(2)}) copy-start(f32[64,1024]{1,0:T(8,128)} %param.20) | copy-start | bytes 786436
  6.5 210.6 %all-gather.2.cloned.1.call-start = ((), (), s32[]{:S(2)}) async-start(), calls=%async_computation.3 | async-start | bytes 2359296 | tf_op jit(solution)/shard_map/all_gather | solution.py:74
  7.8 4.9 %copy-start.6 = (s32[1,4,64]{2,1,0:T(4,128)S(1)}, s32[1,4,64]{2,1,0:T(4,128)}, u32[]{:S(2)}) copy-start(s32[1,4,64]{2,1,0:T(4,128)} %param.16) | copy-start | bytes 3076
  7.8 4.9 %copy-start.7 = (s32[1,4,64]{2,1,0:T(4,128)S(1)}, s32[1,4,64]{2,1,0:T(4,128)}, u32[]{:S(2)}) copy-start(s32[1,4,64]{2,1,0:T(4,128)} %param.15) | copy-start | bytes 3076
  7.9 4.9 %copy-start.5 = (s32[1,4,64]{2,1,0:T(4,128)S(1)}, s32[1,4,64]{2,1,0:T(4,128)}, u32[]{:S(2)}) copy-start(s32[1,4,64]{2,1,0:T(4,128)} %param.14) | copy-start | bytes 3076
  12.8 73.0 %copy-start.4 = (s32[1,1024]{1,0:T(1,128)S(1)}, s32[1,1024]{1,0:T(1,128)}, u32[]{:S(2)}) copy-start(s32[1,1024]{1,0:T(1,128)} %param.17) | copy-start | bytes 12292
  85.8 3.9 %copy-start.3 = (f32[64,1024]{1,0:T(8,128)S(1)}, f32[64,1024]{1,0:T(8,128)}, u32[]{:S(2)}) copy-start(f32[64,1024]{1,0:T(8,128)} %param.19) | copy-start | bytes 786436
  94.5 4.7 %copy-start.2 = (f32[1024,1024]{1,0:T(8,128)S(1)}, f32[1024,1024]{1,0:T(8,128)}, u32[]{:S(2)}) copy-start(f32[1024,1024]{1,0:T(8,128)} %get-tuple-element.99) | copy-start | bytes 12582916
  217.2 34.5 %copy-start.1 = (f32[64,1024]{1,0:T(8,128)S(1)}, f32[64,1024]{1,0:T(8,128)}, u32[]{:S(2)}) copy-start(f32[64,1024]{1,0:T(8,128)} %param.20) | copy-start | bytes 786436
Sparse Core Ops, SparseCore 0:
  125.3 49.6 all-gather.1
where the time goes:
time: 263 us; the launch traced here: 259 us
  matrix products  88.2 us (34%)
  local copies, waits for them, and re-layouts  84.9 us (32%)
  blocking collectives  52.3 us (20%)
  other arithmetic  17.1 us (7%)
  between operations  15.9 us (6%)
    dot_general x1, matrix products, reduce_measured_rows(): jnp.einsum('mqr,mqc->qrc', left_rows, lax.all_gather(right_q, 'mem', axis...  34.5 us
    dot_general x4, matrix products, apply_update(): jnp.dot(columns, row_block, precision=EXACT_ARITHMETIC, preferred_element...  27.2 us
    unnamed x18, local copies, waits for them, and re-layouts  25.6 us
    psum x1, blocking collectives, per_device(): totals = lax.psum(member_mask * weights[0], 'mem')  21.8 us
    while x4, local copies, waits for them, and re-layouts  21.6 us
    dot_general x2, matrix products, transform(): jnp.dot(onehot.T, weighted, precision=EXACT_ARITHMETIC, preferred_element...  13 us
    gather x4, local copies, waits for them, and re-layouts, apply_update(): row_block = jnp.take(matrix, chosen, axis=0)  11.9 us
    gather x4, local copies, waits for them, and re-layouts, apply_update(): jnp.take(matrix, chosen, axis=1) - unit_cols  11.9 us
  transfers between devices with their start and end apart: 1, of which 0 were waited for; matrix products, arithmetic and copies ran while one was open for 18% of the time, Pallas kernels for 0%

commit v1 on v0

v1 whole, which is shorter than its diff:
```python
import functools
import math

import jax
import jax.numpy as jnp
from jax import lax
from jax.experimental import pallas as pl
from jax.experimental.pallas import tpu as pltpu
from jax.sharding import PartitionSpec as P

TIMES = 4096
LANES = 128
F32 = jnp.float32
BF16 = jnp.bfloat16
NN = (((1,), (0,)), ((), ()))
NT = (((1,), (1,)), ((), ()))
TN = (((0,), (0,)), ((), ()))


def split(x):
    hi = x.astype(BF16)
    return hi, (x - hi.astype(F32)).astype(BF16)


def dot(a, b, dims=NN):
    return lax.dot_general(a, b, dims, preferred_element_type=F32)


def dot_exact(a, b, dims=NN):
    return lax.dot_general(a, b, dims, precision=lax.Precision.HIGHEST, preferred_element_type=F32)


def legendre_rows(times, legs):
    x = (2.0 * times + 1.0) * (1.0 / TIMES) - 1.0
    before, now = jnp.ones_like(x), x
    yield before
    yield now * math.sqrt(3.0)
    for d in range(1, legs - 1):
        before, now = now, ((2 * d + 1) / (d + 1)) * (x * now) - (d / (d + 1)) * before
        yield now * math.sqrt(2.0 * (d + 1) + 1.0)


def measure_kernel(
    n_grp, legs, updates,
    perturb, columns, site, time, left_proj, right_proj, weight, routing,
    out, polys, spread,
):
    order = perturb.shape[1]
    sites, width = left_proj.shape
    q = width // legs
    per = q // n_grp
    touched = columns.shape[0]
    rank = touched // updates
    for d, row in enumerate(legendre_rows(time[...].astype(F32), legs)):
        polys[d : d + 1, :] = row
    onehot = (lax.broadcasted_iota(jnp.int32, (sites, order), 0) == site[...]).astype(BF16)
    onehot2 = jnp.concatenate([onehot, onehot], axis=0)
    vectors = []
    for table in (left_proj, right_proj):
        hi, lo = split(table[...])
        spread[...] = dot(jnp.concatenate([hi, lo], axis=0), onehot2, TN)
        total = jnp.zeros((q, order), F32)
        for d in range(legs):
            total = total + spread[d * q : (d + 1) * q, :] * polys[d : d + 1, :]
        vectors.append(total)
    left_vec, right_vec = vectors

    index = columns[:, 0:1]
    gammas = columns[:, 2:3].astype(F32) * jnp.where(columns[:, 1:2] == 1, 0.6, -0.4)
    select = (lax.broadcasted_iota(jnp.int32, (touched, order), 1) == index).astype(BF16)
    p_hi, p_lo = split(perturb[0])
    l_hi, l_lo = split(left_vec)
    r_hi, r_lo = split(right_vec)
    rows = jnp.concatenate([select, r_hi, r_lo], axis=0)
    cols = jnp.concatenate([select, l_hi, l_lo], axis=0)
    by_rows = dot(rows, p_hi) + dot(rows, p_lo)
    by_cols = dot(cols, p_hi, NT) + dot(cols, p_lo, NT)
    p_rows, p_cols = by_rows[:touched], by_cols[:touched]
    g = by_rows[touched : touched + q] + by_rows[touched + q :]
    w = left_vec + by_cols[touched : touched + q] + by_cols[touched + q :]

    def picked(x):
        hi, lo = split(x)
        return dot(hi, select, NT) + dot(lo, select, NT)

    kernel = picked(p_rows)
    overlap = kernel + dot(select, select, NT)
    eye = (
        lax.broadcasted_iota(jnp.int32, (touched, touched), 0)
        == lax.broadcasted_iota(jnp.int32, (touched, touched), 1)
    ).astype(F32)
    s = jnp.zeros((touched, touched), F32)
    for u in range(updates):
        part = slice(u * rank, (u + 1) * rank)
        if u == 0:
            first, second = eye[:, part], eye[part, :]
        else:
            first = eye[:, part] - dot_exact(s, overlap[:, part])
            second = eye[part, :] - dot_exact(kernel[part, :], s)
        s = s + dot_exact(first, gammas[part, :] * second)
    z = dot_exact(picked(w), s, NT)
    v = dot_exact(picked(g), s)
    left_image = w - dot_exact(z, p_cols)
    v_hi, v_lo = split(v)
    right_image = right_vec + g - (dot_exact(v, p_rows) + dot(v_hi, select) + dot(v_lo, select))

    tiles = order // LANES
    site_f, time_f = site[...].astype(F32), time[...].astype(F32)
    for t in range(tiles):
        lanes = slice(t * LANES, (t + 1) * LANES)
        for k in range(n_grp):
            mine = slice(k * per, (k + 1) * per)
            out[k, t * 2 * per : t * 2 * per + per, :] = left_image[mine, lanes]
            out[k, t * 2 * per + per : (t + 1) * 2 * per, :] = right_image[mine, lanes]
            base = tiles * 2 * per
            out[k, base + t : base + t + 1, :] = site_f[:, lanes]
            out[k, base + tiles + t : base + tiles + t + 1, :] = time_f[:, lanes]
    base = tiles * (2 * per + 2)
    for k in range(n_grp):
        out[k, base : base + 4, :] = jnp.full((4, LANES), weight[0], F32)
        out[k, base + 4 : base + 8, :] = jnp.full((4, LANES), routing[0, 0].astype(F32), F32)


def accumulate_kernel(
    legs, per, tiles, blocks,
    gathered, total_in, out, polys, left_rows, right_rows, table, images, right_pair,
):
    n_mem, n_grp = gathered.shape[0], gathered.shape[1]
    walkers = n_mem * n_grp
    pairs = total_in.shape[2] // LANES
    step = pl.program_id(0)
    mem = lax.axis_index("mem")
    meta = tiles * 2 * per
    last = meta + 2 * tiles

    @pl.when(step == 0)
    def _():
        def member(m, carry):
            times = jnp.concatenate(
                [gathered[m, g, meta + tiles : last, :] for g in range(n_grp)], axis=0
            )
            for d, row in enumerate(legendre_rows(times, legs)):
                polys[d * n_grp * tiles : (d + 1) * n_grp * tiles, :] = row
            for g in range(n_grp):
                walker = m * n_grp + g
                own = gathered[m, g, last + 4 : last + 5, :]
                weight = gathered[m, g, last : last + 1, :]
                same = jnp.zeros_like(own)
                for other in range(n_mem):
                    same = same + jnp.where(
                        gathered[other, g, last + 4 : last + 5, :] == own,
                        gathered[other, g, last : last + 1, :],
                        0.0,
                    )
                factor = weight / same
                for t in range(tiles):
                    lanes = slice(t * LANES, (t + 1) * LANES)
                    site = gathered[m, g, meta + t : meta + t + 1, :].astype(jnp.int32)
                    odd, pair = site % 2, site // 2
                    p = polys[pl.ds(g * tiles + t, legs, stride=n_grp * tiles), :]
                    p = jnp.concatenate(
                        [jnp.where(odd == 0, p, 0.0), jnp.where(odd == 1, p, 0.0)], axis=0
                    )
                    p_hi, p_lo = split(p)
                    table[:LANES, lanes] = p_hi
                    table[LANES:, lanes] = p_lo
                    image = gathered[m, g, t * 2 * per : (t + 1) * 2 * per, :]
                    hi = image.astype(BF16).astype(F32)
                    lo = image - hi
                    at = pair == lax.broadcasted_iota(jnp.int32, (pairs, LANES), 0)
                    at_own = pair == mem * blocks + lax.broadcasted_iota(jnp.int32, (8, LANES), 0)
                    half = per * pairs + per * 8
                    for part, value in ((0, hi), (1, lo)):
                        rows = [jnp.where(at, value[per + k : per + k + 1, :], 0.0) for k in range(per)]
                        rows += [jnp.where(at_own, value[k : k + 1, :], 0.0) for k in range(per)]
                        images[part * half : (part + 1) * half, lanes] = jnp.concatenate(
                            rows, axis=0
                        ).astype(BF16)
                half = per * pairs + per * 8
                both = dot(images[...], table[...], NT)
                summed = both[:half, :LANES] + both[:half, LANES:] + both[half:, :LANES]
                for k in range(per):
                    right_rows[pl.ds(k * pairs * walkers + walker, pairs, stride=walkers), :] = (
                        summed[k * pairs : (k + 1) * pairs, :]
                    )
                    for b in range(blocks):
                        at_row = per * pairs + k * 8 + b
                        left_rows[pl.ds((k * blocks + b) * walkers + walker, 1), :] = (
                            summed[at_row : at_row + 1, :] * factor
                        )
            return carry

        lax.fori_loop(0, n_mem, member, 0)

    transfer, block = step // blocks, step % blocks

    @pl.when(block == 0)
    def _():
        for c in range(pairs):
            start = pl.multiple_of((transfer * pairs + c) * walkers, walkers)
            hi, lo = split(right_rows[pl.ds(start, walkers), :])
            lanes = slice(c * LANES, (c + 1) * LANES)
            right_pair[:walkers, lanes] = hi
            right_pair[walkers : 2 * walkers, lanes] = lo
            right_pair[2 * walkers :, lanes] = hi

    start = pl.multiple_of((transfer * blocks + block) * walkers, walkers)
    hi, lo = split(left_rows[pl.ds(start, walkers), :])
    left = jnp.concatenate([hi, hi, lo], axis=0)
    out[0] = total_in[0] + dot(left, right_pair[...], TN)


def gather_payload(payload):
    swapped = lax.all_to_all(payload, "grp", split_axis=0, concat_axis=0, tiled=True)
    return lax.all_gather(swapped, "mem", axis=0)


def per_device(
    n_grp, n_mem,
    perturb, touched_vertex_index, proposed_spin_values, accept,
    vertex_site_index, vertex_time_index, left_proj, right_proj,
    weights, routing, vertex_function_total,
):
    order = perturb.shape[1]
    sites, width = left_proj.shape
    per, rows, cols = vertex_function_total.shape
    legs = cols // sites
    updates, rank = touched_vertex_index.shape[1:]
    tiles = order // LANES
    blocks = rows // LANES
    payload_rows = tiles * (2 * per + 2) + 8
    columns = jnp.stack(
        [touched_vertex_index[0], proposed_spin_values[0], accept[0]], axis=-1
    ).reshape(updates * rank, 3)
    vmem = pl.BlockSpec(memory_space=pltpu.VMEM)
    smem = pl.BlockSpec(memory_space=pltpu.SMEM)
    payload = pl.pallas_call(
        functools.partial(measure_kernel, n_grp, legs, updates),
        out_shape=jax.ShapeDtypeStruct((n_grp, payload_rows, LANES), F32),
        in_specs=[vmem] * 6 + [smem] * 2,
        out_specs=vmem,
        scratch_shapes=[pltpu.VMEM((legs, order), F32), pltpu.VMEM((width, order), F32)],
        compiler_params=pltpu.CompilerParams(vmem_limit_bytes=48 * 2**20),
    )(perturb, columns, vertex_site_index, vertex_time_index, left_proj, right_proj, weights, routing)
    gathered = gather_payload(payload)
    walkers = n_grp * n_mem
    pairs = cols // LANES
    return pl.pallas_call(
        functools.partial(accumulate_kernel, legs, per, tiles, blocks),
        grid=(per * blocks,),
        out_shape=jax.ShapeDtypeStruct(vertex_function_total.shape, F32),
        in_specs=[
            vmem,
            pl.BlockSpec((1, LANES, cols), lambda i: (i // blocks, i % blocks, 0)),
        ],
        out_specs=pl.BlockSpec((1, LANES, cols), lambda i: (i // blocks, i % blocks, 0)),
        scratch_shapes=[
            pltpu.VMEM((legs * n_grp * tiles, LANES), F32),
            pltpu.VMEM((per * blocks * walkers, LANES), F32),
            pltpu.VMEM((per * pairs * walkers, LANES), F32),
            pltpu.VMEM((2 * LANES, order), BF16),
            pltpu.VMEM((2 * (per * pairs + per * 8), order), BF16),
            pltpu.VMEM((3 * walkers, cols), BF16),
        ],
        compiler_params=pltpu.CompilerParams(vmem_limit_bytes=56 * 2**20),
    )(gathered, vertex_function_total)


def solution(mesh):
    in_specs = (
        P(("grp", "mem"), None, None),
        P(("grp", "mem"), None, None),
        P(("grp", "mem"), None, None),
        P(("grp", "mem"), None, None),
        P(("grp", "mem"), None),
        P(("grp", "mem"), None),
        P(),
        P(),
        P(("grp", "mem")),
        P(("grp", "mem"), None),
        P("grp", "mem", None),
    )
    return jax.shard_map(
        functools.partial(per_device, mesh.shape["grp"], mesh.shape["mem"]),
        mesh=mesh, in_specs=in_specs, out_specs=P("grp", "mem", None), check_vma=False,
    )
```

time: 263 us -> 139 us (0.53); the launches traced: 259 us -> 138 us
  matrix products: 88.2 us -> 0 us
  local copies, waits for them, and re-layouts: 84.9 us -> 7.88 us
  Pallas kernels: 0 us -> 62.4 us
  waiting for transfers between devices: 0.04 us -> 43.6 us
  blocking collectives: 52.3 us -> 9.26 us
  other arithmetic: 17.1 us -> 0.01 us
    dot_general x11 -> x0, matrix products: 88.2 us -> none  [the longest x1 34.5 us: reduce_measured_rows(): jnp.einsum('mqr,mqc->qrc', left_rows, lax.all_gather(right_q, 'mem', axis...]
    pallas_call x0 -> x2, Pallas kernels: none -> 62.4 us  [the longest x1 52.5 us: per_device(): pl.pallas_call(functools.partial(accumulate_kernel, legs, per, tiles, blo...]
    all_gather x1, waiting for transfers between devices: 0.02 us -> 43.6 us  [gather_payload(): return lax.all_gather(swapped, 'mem', axis=0)]
    gather x8 -> x0, local copies, waits for them, and re-layouts: 23.9 us -> none  [the longest x4 11.9 us: apply_update(): row_block = jnp.take(matrix, chosen, axis=0)]
    psum x1 -> x0, blocking collectives: 21.8 us -> none  [per_device(): totals = lax.psum(member_mask * weights[0], 'mem')]
    while x4 -> x0, local copies, waits for them, and re-layouts: 21.6 us -> none
    all_to_all x3 -> x1, blocking collectives: 30.5 us -> 9.26 us  [gather_payload(): lax.all_to_all(payload, 'grp', split_axis=0, concat_axis=0, tiled=True)]
    unnamed x18 -> x10, local copies, waits for them, and re-layouts: 25.6 us -> 5.46 us
  transfers between devices with their start and end apart: 1 -> 1, of which waited for: 0 -> 1; matrix products, arithmetic and copies ran while one was open for 18% -> 0% of each run, Pallas kernels for 0% -> 0%
where the time goes in v1:
time: 139 us; the launch traced here: 138 us
  Pallas kernels  62.4 us (45%)
  waiting for transfers between devices  43.6 us (31%)
  between operations  14.7 us (11%)
  blocking collectives  9.26 us (7%)
  local copies, waits for them, and re-layouts  7.88 us (6%)
    pallas_call x1, Pallas kernels, per_device(): pl.pallas_call(functools.partial(accumulate_kernel, legs, per, tiles, blo...  52.5 us
    all_gather x1, waiting for transfers between devices, gather_payload(): return lax.all_gather(swapped, 'mem', axis=0)  43.6 us
    pallas_call x1, Pallas kernels, per_device(): pl.pallas_call(functools.partial(measure_kernel, n_grp, legs, updates), o...  9.91 us
    all_to_all x1, blocking collectives, gather_payload(): lax.all_to_all(payload, 'grp', split_axis=0, concat_axis=0, tiled=True)  9.26 us
    unnamed x10, local copies, waits for them, and re-layouts  5.46 us
  transfers between devices with their start and end apart: 1, of which 1 were waited for; matrix products, arithmetic and copies ran while one was open for 0% of the time, Pallas kernels for 0%

profile of v1, /device:TPU:0, one launch (start us, length us, event | category | flops | bytes accessed | tf_op | source)
XLA Modules:
  0.0 137.9 jit_solution(14642367981055755745)
XLA Ops:
  6.5 0.0 all-gather.3.cloned.1.call-start
  7.8 0.8 stack.9
  8.6 0.8 stack.10
  9.4 0.8 stack.11
  10.1 0.1 copy.15.columns
  10.3 0.0 copy-start
  10.3 2.2 %copy-done = f32[1,1024,1024]{2,1,0:T(8,128)S(1)} copy-done((f32[1,1024,1024]{2,1,0:T(8,128)S(1)}, f32[1,1024,1024]{2,1,0:T(8,128)}, u32[]{:S(2)}) %copy-start) | copy-done | bytes 4194328
  12.5 0.0 copy-start.1
  12.5 0.9 copy-done.1
  13.4 0.0 copy-start.2
  13.4 0.9 copy-done.2
  14.4 0.0 copy-start.3
  14.4 0.7 copy-done.3
  15.1 0.0 copy-start.4
  15.1 0.7 copy-done.4
  15.7 9.9 %shard_map.109 = f32[4,88,128]{2,1,0:T(8,128)S(1)} custom-call(f32[1,1024,1024]{2,1,0:T(8,128)S(1)} %copy-done, s32[256,3]{1,0:T(8,128)S(1)} %copy.15.columns, s32[1,1024]{1,0:T(1,128)S(1)} %copy-done.3, s32[1,1024]{1,0:T(1,128)S(1)} %copy-done.4, f32[64,1024]{1,0:T(8,128)S(1)} %copy-done.1, f32[64,1024]{1,0:T(8,128)S(1)} %copy-done.2, f32[1]{0:T(128)S(6)} %copy.16.weight, ...), custom_call_target="tpu_custom_call" | custom-call | tf_op jit(solution)/shard_map/pallas_call | solution.py:237
  25.7 9.3 %all_to_all.5 = f32[4,88,128]{2,1,0:T(8,128)} all-to-all(f32[4,88,128]{2,1,0:T(8,128)S(1)} %shard_map.109), channel_id=1, replica_groups=mesh['grp'=4,'mem'=8] {'grp'}, dimensions={0} | all-to-all | bytes 360448 | tf_op jit(solution)/shard_map/all_to_all | solution.py:214
  34.9 0.0 all-gather.3.cloned.1.call-update
  34.9 43.6 %all-gather.3.cloned.1.call-done = f32[32,88,128]{2,1,0:T(8,128)} async-done(((f32[4,88,128]{2,1,0:T(8,128)}), f32[32,88,128]{2,1,0:T(8,128)}) %all-gather.3.cloned.1.call-update) | async-done | bytes 1441808 | tf_op jit(solution)/shard_map/all_gather | solution.py:215
  78.6 52.5 %shard_map.110 = f32[4,512,4096]{2,1,0:T(8,128)} custom-call(f32[8,4,88,128]{3,2,1,0:T(8,128)} %bitcast.1, f32[4,512,4096]{2,1,0:T(8,128)} %total_in.1), custom_call_target="tpu_custom_call" | custom-call | tf_op jit(solution)/shard_map/pallas_call | solution.py:248
  (1 shorter events, 0.0 us)
Async XLA Ops:
  6.5 72.0 %all-gather.3.cloned.1.call-start = ((), (), s32[]{:S(2)}) async-start(), calls=%async_computation.1 | async-start | bytes 1622016 | tf_op jit(solution)/shard_map/all_gather | solution.py:215
  10.3 2.2 %copy-start = (f32[1,1024,1024]{2,1,0:T(8,128)S(1)}, f32[1,1024,1024]{2,1,0:T(8,128)}, u32[]{:S(2)}) copy-start(f32[1,1024,1024]{2,1,0:T(8,128)} %perturb.1) | copy-start | bytes 12582916
  12.5 0.9 copy-start.1
  13.4 0.9 copy-start.2
  14.4 0.7 copy-start.3
  15.1 0.7 copy-start.4
Sparse Core Ops, SparseCore 0:
  35.1 43.4 all-gather.2

commit v2 on v1

--- a/solution.py
+++ b/solution.py
@@ -14,6 +14,7 @@
 BF16 = jnp.bfloat16
 NN = (((1,), (0,)), ((), ()))
 NT = (((1,), (1,)), ((), ()))
+MESH = pl.DeviceIdType.MESH
 TN = (((0,), (0,)), ((), ()))
 
 
@@ -42,15 +43,24 @@
 
 def measure_kernel(
     n_grp, legs, updates,
-    perturb, columns, site, time, left_proj, right_proj, weight, routing,
-    out, polys, spread,
+    perturb_in, touched_in, spins_in, accept_in, site_in, time_in, left_in, right_in, weight, routing,
+    out, polys, spread, perturb, chosen, spins, accept, site, time, left_proj, right_proj, arrived,
 ):
+    loads = []
+    for k, (source, target) in enumerate((
+        (time_in, time), (site_in, site), (left_in, left_proj), (right_in, right_proj),
+        (touched_in, chosen), (spins_in, spins), (accept_in, accept), (perturb_in, perturb),
+    )):
+        loads.append(pltpu.make_async_copy(source, target, arrived.at[k]))
+        loads[-1].start()
     order = perturb.shape[1]
     sites, width = left_proj.shape
     q = width // legs
     per = q // n_grp
-    touched = columns.shape[0]
-    rank = touched // updates
+    rank = chosen.shape[2]
+    touched = updates * rank
+    for load in loads[:4]:
+        load.wait()
     for d, row in enumerate(legendre_rows(time[...].astype(F32), legs)):
         polys[d : d + 1, :] = row
     onehot = (lax.broadcasted_iota(jnp.int32, (sites, order), 0) == site[...]).astype(BF16)
@@ -65,8 +75,21 @@
         vectors.append(total)
     left_vec, right_vec = vectors
 
-    index = columns[:, 0:1]
-    gammas = columns[:, 2:3].astype(F32) * jnp.where(columns[:, 1:2] == 1, 0.6, -0.4)
+    for load in loads[4:]:
+        load.wait()
+    square = lax.broadcasted_iota(jnp.int32, (rank, rank), 0) == lax.broadcasted_iota(
+        jnp.int32, (rank, rank), 1
+    )
+
+    def column(rows):
+        parts = [
+            jnp.sum(jnp.where(square, rows[u : u + 1, :].astype(F32), 0.0), axis=1, keepdims=True)
+            for u in range(updates)
+        ]
+        return jnp.concatenate(parts, axis=0)
+
+    index = column(chosen[0]).astype(jnp.int32)
+    gammas = column(accept[0].astype(F32) * jnp.where(spins[0] == 1, 0.6, -0.4))
     select = (lax.broadcasted_iota(jnp.int32, (touched, order), 1) == index).astype(BF16)
     p_hi, p_lo = split(perturb[0])
     l_hi, l_lo = split(left_vec)
@@ -123,18 +146,25 @@
 
 def accumulate_kernel(
     legs, per, tiles, blocks,
-    gathered, total_in, out, polys, left_rows, right_rows, table, images, right_pair,
+    gathered, total_hbm, out, polys, left_rows, right_rows, table, images, right_pair, held, arrived,
 ):
     n_mem, n_grp = gathered.shape[0], gathered.shape[1]
     walkers = n_mem * n_grp
-    pairs = total_in.shape[2] // LANES
+    pairs = total_hbm.shape[2] // LANES
     step = pl.program_id(0)
     mem = lax.axis_index("mem")
     meta = tiles * 2 * per
     last = meta + 2 * tiles
 
+    def load(at):
+        k, b = at // blocks, at % blocks
+        rows = pl.ds(pl.multiple_of(b * LANES, LANES), LANES)
+        return pltpu.make_async_copy(total_hbm.at[k, rows, :], held.at[at], arrived.at[at])
+
     @pl.when(step == 0)
     def _():
+        lax.fori_loop(0, per * blocks, lambda at, carry: (load(at).start(), carry)[1], 0)
+
         def member(m, carry):
             times = jnp.concatenate(
                 [gathered[m, g, meta + tiles : last, :] for g in range(n_grp)], axis=0
@@ -207,12 +237,105 @@
     start = pl.multiple_of((transfer * blocks + block) * walkers, walkers)
     hi, lo = split(left_rows[pl.ds(start, walkers), :])
     left = jnp.concatenate([hi, hi, lo], axis=0)
-    out[0] = total_in[0] + dot(left, right_pair[...], TN)
-
-
-def gather_payload(payload):
-    swapped = lax.all_to_all(payload, "grp", split_axis=0, concat_axis=0, tiled=True)
-    return lax.all_gather(swapped, "mem", axis=0)
+    load(step).wait()
+    out[0] = held[step] + dot(left, right_pair[...], TN)
+
+
+def gather_kernel(n_grp, n_mem, payload, out, grp_send, grp_recv, ring_send, ring_recv, own_sem):
+    grp, mem = lax.axis_index("grp"), lax.axis_index("mem")
+    half = n_mem // 2
+
+    def at_place(place):
+        return jnp.where(place < half, 2 * place, 2 * (n_mem - 1 - place) + 1)
+
+    place = jnp.where(mem % 2 == 0, mem // 2, n_mem - 1 - mem // 2)
+    peers = [
+        ((grp // 2 + j // 2) % (n_grp // 2)) * 2 + (grp % 2 + j % 2) % 2 for j in range(n_grp)
+    ]
+    sides = [at_place((place + 1) % n_mem), at_place((place + n_mem - 1) % n_mem)]
+
+    barrier = pltpu.get_barrier_semaphore()
+    for peer in peers[1:]:
+        pl.semaphore_signal(barrier, inc=1, device_id=(peer, mem), device_id_type=MESH)
+    for side in sides:
+        pl.semaphore_signal(barrier, inc=1, device_id=(grp, side), device_id_type=MESH)
+    pl.semaphore_wait(barrier, n_grp + 1)
+
+    def runs(step, j):
+        if step < half - 1:
+            return (0, 1)
+        if step == half - 1:
+            return (j % 2,)
+        return ()
+
+    started = []
+
+    def pass_on(step, j, side, source):
+        origin = at_place((place + (n_mem - step if side == 0 else step)) % n_mem)
+        copy = pltpu.make_async_remote_copy(
+            src_ref=payload.at[peers[j]] if source is None else source,
+            dst_ref=out.at[origin, peers[j]],
+            send_sem=ring_send.at[side, step, j],
+            recv_sem=ring_recv.at[side, step, j],
+            device_id=(grp, sides[side]),
+            device_id_type=MESH,
+        )
+        copy.start()
+        started.append(copy)
+
+    crossing = []
+    for j in range(1, n_grp):
+        copy = pltpu.make_async_remote_copy(
+            src_ref=payload.at[peers[j]],
+            dst_ref=out.at[mem, grp],
+            send_sem=grp_send.at[peers[j]],
+            recv_sem=grp_recv.at[grp],
+            device_id=(peers[j], mem),
+            device_id_type=MESH,
+        )
+        copy.start()
+        crossing.append(copy)
+    for side in runs(0, 0):
+        pass_on(0, 0, side, None)
+    own = pltpu.make_async_copy(payload.at[grp], out.at[mem, grp], own_sem)
+    own.start()
+    for j in range(1, n_grp):
+        block = out.at[mem, peers[j]]
+        pltpu.make_async_copy(block, block, grp_recv.at[peers[j]]).wait()
+        for side in runs(0, j):
+            pass_on(0, j, side, block)
+    for step in range(1, half + 1):
+        for j in range(n_grp):
+            for side in runs(step - 1, j):
+                origin = at_place((place + (n_mem - step if side == 0 else step)) % n_mem)
+                block = out.at[origin, peers[j]]
+                pltpu.make_async_copy(block, block, ring_recv.at[side, step - 1, j]).wait()
+                if side in runs(step, j):
+                    pass_on(step, j, side, block)
+    own.wait()
+    for copy in crossing + started:
+        copy.wait_send()
+
+
+def gather_payload(payload, n_grp, n_mem):
+    half = n_mem // 2
+    vmem = pl.BlockSpec(memory_space=pltpu.VMEM)
+    return pl.pallas_call(
+        functools.partial(gather_kernel, n_grp, n_mem),
+        out_shape=jax.ShapeDtypeStruct((n_mem, *payload.shape), F32),
+        in_specs=[vmem],
+        out_specs=vmem,
+        scratch_shapes=[
+            pltpu.SemaphoreType.DMA((n_grp,)),
+            pltpu.SemaphoreType.DMA((n_grp,)),
+            pltpu.SemaphoreType.DMA((2, half, n_grp)),
+            pltpu.SemaphoreType.DMA((2, half, n_grp)),
+            pltpu.SemaphoreType.DMA,
+        ],
+        compiler_params=pltpu.CompilerParams(
+            collective_id=0, has_side_effects=True, vmem_limit_bytes=(20 if n_mem > 8 else 8) * 2**20
+        ),
+    )(payload)
 
 
 def per_device(
@@ -229,30 +352,31 @@
     tiles = order // LANES
     blocks = rows // LANES
     payload_rows = tiles * (2 * per + 2) + 8
-    columns = jnp.stack(
-        [touched_vertex_index[0], proposed_spin_values[0], accept[0]], axis=-1
-    ).reshape(updates * rank, 3)
     vmem = pl.BlockSpec(memory_space=pltpu.VMEM)
     smem = pl.BlockSpec(memory_space=pltpu.SMEM)
+    hbm = pl.BlockSpec(memory_space=pl.ANY)
+    loaded = (
+        perturb, touched_vertex_index, proposed_spin_values, accept,
+        vertex_site_index, vertex_time_index, left_proj, right_proj,
+    )
     payload = pl.pallas_call(
         functools.partial(measure_kernel, n_grp, legs, updates),
         out_shape=jax.ShapeDtypeStruct((n_grp, payload_rows, LANES), F32),
-        in_specs=[vmem] * 6 + [smem] * 2,
+        in_specs=[hbm] * 8 + [smem] * 2,
         out_specs=vmem,
-        scratch_shapes=[pltpu.VMEM((legs, order), F32), pltpu.VMEM((width, order), F32)],
+        scratch_shapes=[pltpu.VMEM((legs, order), F32), pltpu.VMEM((width, order), F32)]
+        + [pltpu.VMEM(x.shape, x.dtype) for x in loaded]
+        + [pltpu.SemaphoreType.DMA((len(loaded),))],
         compiler_params=pltpu.CompilerParams(vmem_limit_bytes=48 * 2**20),
-    )(perturb, columns, vertex_site_index, vertex_time_index, left_proj, right_proj, weights, routing)
-    gathered = gather_payload(payload)
+    )(*loaded, weights, routing)
+    gathered = gather_payload(payload, n_grp, n_mem)
     walkers = n_grp * n_mem
     pairs = cols // LANES
     return pl.pallas_call(
         functools.partial(accumulate_kernel, legs, per, tiles, blocks),
         grid=(per * blocks,),
         out_shape=jax.ShapeDtypeStruct(vertex_function_total.shape, F32),
-        in_specs=[
-            vmem,
-            pl.BlockSpec((1, LANES, cols), lambda i: (i // blocks, i % blocks, 0)),
-        ],
+        in_specs=[vmem, hbm],
         out_specs=pl.BlockSpec((1, LANES, cols), lambda i: (i // blocks, i % blocks, 0)),
         scratch_shapes=[
             pltpu.VMEM((legs * n_grp * tiles, LANES), F32),
@@ -261,6 +385,8 @@
             pltpu.VMEM((2 * LANES, order), BF16),
             pltpu.VMEM((2 * (per * pairs + per * 8), order), BF16),
             pltpu.VMEM((3 * walkers, cols), BF16),
+            pltpu.VMEM((per * blocks, LANES, cols), F32),
+            pltpu.SemaphoreType.DMA((per * blocks,)),
         ],
         compiler_params=pltpu.CompilerParams(vmem_limit_bytes=56 * 2**20),
     )(gathered, vertex_function_total)

time: 139 us -> 83.8 us (0.60)
  waiting for transfers between devices: 43.6 us -> 0 us
  between operations: 14.7 us -> 1.34 us
  Pallas kernels: 62.4 us -> 73.5 us
  blocking collectives: 9.26 us -> 0 us
    all_gather x1 -> x0, waiting for transfers between devices: 43.6 us -> none  [gather_payload(): return lax.all_gather(swapped, 'mem', axis=0)]
    pallas_call x0 -> x1, Pallas kernels: none -> 23.7 us  [gather_payload(): pl.pallas_call(functools.partial(gather_kernel, n_grp, n_mem), out_shape=...]
    pallas_call x1, Pallas kernels: 52.5 us -> 39.2 us  [per_device(): pl.pallas_call(functools.partial(accumulate_kernel, legs, per, tiles, blo...]
    all_to_all x1 -> x0, blocking collectives: 9.26 us -> none  [gather_payload(): lax.all_to_all(payload, 'grp', split_axis=0, concat_axis=0, tiled=True)]
    unnamed x10 -> x18, local copies, waits for them, and re-layouts: 5.46 us -> 8.6 us
    another operation x4 -> x0, local copies, waits for them, and re-layouts: 2.42 us -> none  [per_device(): jnp.stack([touched_vertex_index[0], proposed_spin_values[0], accept[0]],...]
  transfers between devices with their start and end apart: 1 -> 0, of which waited for: 1 -> 0; matrix products, arithmetic and copies ran while one was open for 0% -> 0% of each run, Pallas kernels for 0% -> 0%
where the time goes in v2:
time: 83.8 us; the launch traced here: 83.4 us
  Pallas kernels  73.5 us (88%)
  local copies, waits for them, and re-layouts  8.6 us (10%)
  between operations  1.34 us (2%)
    pallas_call x1, Pallas kernels, per_device(): pl.pallas_call(functools.partial(accumulate_kernel, legs, per, tiles, blo...  39.2 us
    pallas_call x1, Pallas kernels, gather_payload(): pl.pallas_call(functools.partial(gather_kernel, n_grp, n_mem), out_shape=...  23.7 us
    pallas_call x1, Pallas kernels, per_device(): pl.pallas_call(functools.partial(measure_kernel, n_grp, legs, updates), o...  10.6 us
    unnamed x18, local copies, waits for them, and re-layouts  8.6 us

profile of v2, /device:TPU:0, one launch (start us, length us, event | category | flops | bytes accessed | tf_op | source)
XLA Modules:
  0.0 83.4 jit_solution(3027330701971953446)
XLA Ops:
  1.3 0.0 copy-start.1
  1.3 2.2 %copy-done.1 = f32[1,1024,1024]{2,1,0:T(8,128)S(1)} copy-done((f32[1,1024,1024]{2,1,0:T(8,128)S(1)}, f32[1,1024,1024]{2,1,0:T(8,128)}, u32[]{:S(2)}) %copy-start.1) | copy-done | bytes 4194328
  3.5 0.0 copy-start.2
  3.5 0.9 %copy-done.2 = f32[64,1024]{1,0:T(8,128)S(1)} copy-done((f32[64,1024]{1,0:T(8,128)S(1)}, f32[64,1024]{1,0:T(8,128)}, u32[]{:S(2)}) %copy-start.2) | copy-done | bytes 262168
  4.4 0.0 copy-start.3
  4.4 0.9 %copy-done.3 = f32[64,1024]{1,0:T(8,128)S(1)} copy-done((f32[64,1024]{1,0:T(8,128)S(1)}, f32[64,1024]{1,0:T(8,128)}, u32[]{:S(2)}) %copy-start.3) | copy-done | bytes 262168
  5.4 0.0 copy-start.4
  5.4 0.7 copy-done.4
  6.1 0.0 copy-start.5
  6.1 0.7 copy-done.5
  6.8 0.0 copy-start.6
  6.8 0.7 copy-done.6
  7.4 0.0 copy-start.7
  7.4 0.7 copy-done.7
  8.1 0.0 copy-start.8
  8.1 0.7 copy-done.8
  8.8 10.6 %shard_map.109.payload = f32[4,88,128]{2,1,0:T(8,128)S(1)} custom-call(f32[1,1024,1024]{2,1,0:T(8,128)S(1)} %copy-done.1, s32[1,4,64]{2,1,0:T(4,128)S(1)} %copy-done.6, s32[1,4,64]{2,1,0:T(4,128)S(1)} %copy-done.7, s32[1,4,64]{2,1,0:T(4,128)S(1)} %copy-done.8, s32[1,1024]{1,0:T(1,128)S(1)} %copy-done.4, s32[1,1024]{1,0:T(1,128)S(1)} %copy-done.5, ...), custom_call_target="tpu_custom_call" | custom-call | tf_op jit(solution)/shard_map/pallas_call | solution.py:362
  19.4 23.7 %shard_map.110.gathered = f32[8,4,88,128]{3,2,1,0:T(8,128)S(1)} custom-call(f32[4,88,128]{2,1,0:T(8,128)S(1)} %shard_map.109.payload), custom_call_target="tpu_custom_call" | custom-call | tf_op jit(solution)/shard_map/pallas_call | solution.py:323
  43.1 0.0 copy-start
  43.1 1.1 %copy-done = f32[8,4,88,128]{3,2,1,0:T(8,128)} copy-done((f32[8,4,88,128]{3,2,1,0:T(8,128)}, f32[8,4,88,128]{3,2,1,0:T(8,128)S(1)}, u32[]{:S(2)}) %copy-start) | copy-done | bytes 1441816
  44.2 39.2 %shard_map.111 = f32[4,512,4096]{2,1,0:T(8,128)} custom-call(f32[8,4,88,128]{3,2,1,0:T(8,128)} %copy-done, f32[4,512,4096]{2,1,0:T(8,128)} %total_hbm.1), custom_call_target="tpu_custom_call" | custom-call | tf_op jit(solution)/shard_map/pallas_call | solution.py:375
Async XLA Ops:
  1.3 2.2 %copy-start.1 = (f32[1,1024,1024]{2,1,0:T(8,128)S(1)}, f32[1,1024,1024]{2,1,0:T(8,128)}, u32[]{:S(2)}) copy-start(f32[1,1024,1024]{2,1,0:T(8,128)} %perturb_in.1) | copy-start | bytes 12582916
  3.5 0.9 %copy-start.2 = (f32[64,1024]{1,0:T(8,128)S(1)}, f32[64,1024]{1,0:T(8,128)}, u32[]{:S(2)}) copy-start(f32[64,1024]{1,0:T(8,128)} %left_in.1) | copy-start | bytes 786436
  4.4 0.9 %copy-start.3 = (f32[64,1024]{1,0:T(8,128)S(1)}, f32[64,1024]{1,0:T(8,128)}, u32[]{:S(2)}) copy-start(f32[64,1024]{1,0:T(8,128)} %right_in.1) | copy-start | bytes 786436
  5.4 0.7 copy-start.4
  6.1 0.7 copy-start.5
  6.8 0.7 copy-start.6
  7.4 0.7 copy-start.7
  8.1 0.7 copy-start.8
  43.1 1.1 %copy-start = (f32[8,4,88,128]{3,2,1,0:T(8,128)}, f32[8,4,88,128]{3,2,1,0:T(8,128)S(1)}, u32[]{:S(2)}) copy-start(f32[8,4,88,128]{3,2,1,0:T(8,128)S(1)} %shard_map.110.gathered) | copy-start | bytes 4325380

commit v3 on v2

--- a/solution.py
+++ b/solution.py
@@ -192,8 +192,8 @@
                         [jnp.where(odd == 0, p, 0.0), jnp.where(odd == 1, p, 0.0)], axis=0
                     )
                     p_hi, p_lo = split(p)
-                    table[:LANES, lanes] = p_hi
-                    table[LANES:, lanes] = p_lo
+                    table[g % 2, :LANES, lanes] = p_hi
+                    table[g % 2, LANES:, lanes] = p_lo
                     image = gathered[m, g, t * 2 * per : (t + 1) * 2 * per, :]
                     hi = image.astype(BF16).astype(F32)
                     lo = image - hi
@@ -203,11 +203,11 @@
                     for part, value in ((0, hi), (1, lo)):
                         rows = [jnp.where(at, value[per + k : per + k + 1, :], 0.0) for k in range(per)]
                         rows += [jnp.where(at_own, value[k : k + 1, :], 0.0) for k in range(per)]
-                        images[part * half : (part + 1) * half, lanes] = jnp.concatenate(
+                        images[g % 2, part * half : (part + 1) * half, lanes] = jnp.concatenate(
                             rows, axis=0
                         ).astype(BF16)
                 half = per * pairs + per * 8
-                both = dot(images[...], table[...], NT)
+                both = dot(images[g % 2], table[g % 2], NT)
                 summed = both[:half, :LANES] + both[:half, LANES:] + both[half:, :LANES]
                 for k in range(per):
                     right_rows[pl.ds(k * pairs * walkers + walker, pairs, stride=walkers), :] = (
@@ -323,7 +323,7 @@
     return pl.pallas_call(
         functools.partial(gather_kernel, n_grp, n_mem),
         out_shape=jax.ShapeDtypeStruct((n_mem, *payload.shape), F32),
-        in_specs=[vmem],
+        in_specs=[pl.BlockSpec(memory_space=pl.ANY)],
         out_specs=vmem,
         scratch_shapes=[
             pltpu.SemaphoreType.DMA((n_grp,)),
@@ -367,7 +367,7 @@
         scratch_shapes=[pltpu.VMEM((legs, order), F32), pltpu.VMEM((width, order), F32)]
         + [pltpu.VMEM(x.shape, x.dtype) for x in loaded]
         + [pltpu.SemaphoreType.DMA((len(loaded),))],
-        compiler_params=pltpu.CompilerParams(vmem_limit_bytes=48 * 2**20),
+        compiler_params=pltpu.CompilerParams(vmem_limit_bytes=67043328),
     )(*loaded, weights, routing)
     gathered = gather_payload(payload, n_grp, n_mem)
     walkers = n_grp * n_mem
@@ -382,13 +382,13 @@
             pltpu.VMEM((legs * n_grp * tiles, LANES), F32),
             pltpu.VMEM((per * blocks * walkers, LANES), F32),
             pltpu.VMEM((per * pairs * walkers, LANES), F32),
-            pltpu.VMEM((2 * LANES, order), BF16),
-            pltpu.VMEM((2 * (per * pairs + per * 8), order), BF16),
+            pltpu.VMEM((2, 2 * LANES, order), BF16),
+            pltpu.VMEM((2, 2 * (per * pairs + per * 8), order), BF16),
             pltpu.VMEM((3 * walkers, cols), BF16),
             pltpu.VMEM((per * blocks, LANES, cols), F32),
             pltpu.SemaphoreType.DMA((per * blocks,)),
         ],
-        compiler_params=pltpu.CompilerParams(vmem_limit_bytes=56 * 2**20),
+        compiler_params=pltpu.CompilerParams(vmem_limit_bytes=50 * 2**20),
     )(gathered, vertex_function_total)
 
 

time: 83.8 us -> 77.6 us (0.926)
  local copies, waits for them, and re-layouts: 8.6 us -> 0.92 us
  Pallas kernels: 73.5 us -> 75.2 us
    unnamed x18 -> x2, local copies, waits for them, and re-layouts: 8.6 us -> 0.92 us
    pallas_call x1, Pallas kernels: 10.6 us -> 12.1 us  [per_device(): pl.pallas_call(functools.partial(measure_kernel, n_grp, legs, updates), o...]
where the time goes in v3:
time: 77.6 us; the launch traced here: 77.4 us
  Pallas kernels  75.2 us (97%)
  between operations  1.32 us (2%)
  local copies, waits for them, and re-layouts  0.92 us (1%)
    pallas_call x1, Pallas kernels, per_device(): pl.pallas_call(functools.partial(accumulate_kernel, legs, per, tiles, blo...  39.6 us
    pallas_call x1, Pallas kernels, gather_payload(): pl.pallas_call(functools.partial(gather_kernel, n_grp, n_mem), out_shape=...  23.6 us
    pallas_call x1, Pallas kernels, per_device(): pl.pallas_call(functools.partial(measure_kernel, n_grp, legs, updates), o...  12.1 us

profile of v3, /device:TPU:0, one launch (start us, length us, event | category | flops | bytes accessed | tf_op | source)
XLA Modules:
  0.0 77.4 jit_solution(11833339677599276439)
XLA Ops:
  1.3 12.1 %shard_map.109.payload = f32[4,88,128]{2,1,0:T(8,128)} custom-call(f32[1,1024,1024]{2,1,0:T(8,128)} %perturb_in.1, s32[1,4,64]{2,1,0:T(4,128)} %touched_in.1, s32[1,4,64]{2,1,0:T(4,128)} %spins_in.1, s32[1,4,64]{2,1,0:T(4,128)} %accept_in.1, s32[1,1024]{1,0:T(1,128)} %site_in.1, s32[1,1024]{1,0:T(1,128)} %time_in.1, f32[64,1024]{1,0:T(8,128)} %left_in.1, ...), custom_call_target="tpu_custom_call" | custom-call | tf_op jit(solution)/shard_map/pallas_call | solution.py:362
  13.4 0.0 copy-start
  13.4 0.9 %copy-done = f32[4,88,128]{2,1,0:T(8,128)S(1)} copy-done((f32[4,88,128]{2,1,0:T(8,128)S(1)}, f32[4,88,128]{2,1,0:T(8,128)}, u32[]{:S(2)}) %copy-start) | copy-done | bytes 180248
  14.3 23.6 %shard_map.110.gathered = f32[8,4,88,128]{3,2,1,0:T(8,128)S(1)} custom-call(f32[4,88,128]{2,1,0:T(8,128)S(1)} %copy-done), custom_call_target="tpu_custom_call" | custom-call | tf_op jit(solution)/shard_map/pallas_call | solution.py:323
  37.9 39.6 %shard_map.111 = f32[4,512,4096]{2,1,0:T(8,128)} custom-call(f32[8,4,88,128]{3,2,1,0:T(8,128)S(1)} %shard_map.110.gathered, f32[4,512,4096]{2,1,0:T(8,128)} %total_hbm.1), custom_call_target="tpu_custom_call" | custom-call | tf_op jit(solution)/shard_map/pallas_call | solution.py:375
Async XLA Ops:
  13.4 0.9 %copy-start = (f32[4,88,128]{2,1,0:T(8,128)S(1)}, f32[4,88,128]{2,1,0:T(8,128)}, u32[]{:S(2)}) copy-start(f32[4,88,128]{2,1,0:T(8,128)} %shard_map.109.payload) | copy-start | bytes 540676
